TPU v7x, 512 devices: a whole 4x8x8 slice. The times are simulated.
512 devices in a mesh: seq: 64 (over x, y, core), chan: 8 (over z).
Axes of the slice: x: 4, y: 8, z: 8, core: 2. Of those that a mesh axis runs over, the one named last changes fastest.
Arguments:
- gate_outer: bfloat16 [8192, 4096], P('seq', 'chan'), may hold values from -520 to 520
- gate_inner: bfloat16 [8192, 4096], P('seq', 'chan'), may hold values from -6 to 6
- value_in: bfloat16 [8192, 4096], P('seq', 'chan'), may hold values from -6 to 6
- pole_rates: float32 [8, 4096], P(None, 'chan'), may hold values from 0 to 1, as said below
- pole_weights: float32 [8, 4096], P(None, 'chan'), may hold values from -4 to 4
- skip_gain: float32 [4096], P('chan'), may hold values from -1 to 1
- query_rows: bfloat16 [8192, 4096], P('seq', 'chan'), may hold values from -6 to 6
- key_rows: bfloat16 [8192, 4096], P('seq', 'chan'), may hold values from -6 to 6
Outputs:
- mixed: bfloat16 [8192, 4096], P('seq', 'chan')
Inputs may be any that keep to these rules, and one draw needn't show every extreme that they name: `pole_rates`: each rate is positive and at most 1/30.
All inputs are finite; a program needn't handle non-finite values.
Results may differ from a plain program's by a relative error of at most 0.0065.
Values may be sent and summed in bfloat16 or wider, within the bound.
A program may use at most 128 MiB of HBM per device.

v0:
```python
import math
import jax
import jax.numpy as jnp
from jax import lax
from jax.sharding import PartitionSpec as P

HD = 128


def prefix(part, axis, combine, identity):
    place = lax.axis_index(axis)
    gathered = jax.tree.map(lambda a: lax.all_gather(a, axis), part)
    state = jax.tree.map(lambda a, e: jnp.zeros_like(a) + jnp.asarray(e, a.dtype), part, identity)

    def one(turn, state):
        return combine(
            state, jax.tree.map(lambda a: lax.dynamic_index_in_dim(a, turn, 0, False), gathered)
        )

    return lax.fori_loop(0, place, one, state)


def block_update(carried, queries, query_pos, key_part, value_part, key_start, score_scale):
    run_max, run_sum, run_acc = carried
    heads_here = run_max.shape[0]
    key_count = key_part.shape[0]
    query_heads = queries.reshape(queries.shape[0], heads_here, -1)
    key_heads = key_part.reshape(key_count, heads_here, -1)
    value_heads = value_part.reshape(key_count, heads_here, -1)
    scores = (
        jnp.einsum("qhd,khd->hqk", query_heads, key_heads, preferred_element_type=jnp.float32)
        * score_scale
    )
    key_pos = key_start + jnp.arange(key_count, dtype=jnp.int32)
    visible = key_pos[None, None, :] <= query_pos[None, :, None]
    scores = jnp.where(visible, scores, -1e30)
    new_max = jnp.maximum(run_max, jnp.max(scores, axis=2))
    rescale = jnp.exp(run_max - new_max)
    expo = jnp.where(visible, jnp.exp(scores - new_max[:, :, None]), 0.0)
    new_sum = run_sum * rescale + jnp.sum(expo, axis=2)
    new_acc = run_acc * rescale[:, :, None] + jnp.einsum(
        "hqk,khd->hqd", expo.astype(jnp.bfloat16), value_heads, preferred_element_type=jnp.float32
    )
    return (new_max, new_sum, new_acc)


def fold_keys(carried, queries, query_pos, pieces, score_scale):
    key_piece, value_piece = pieces
    count_rows = key_piece.shape[0]
    step_rows = math.gcd(count_rows, 1024)

    def one_step(step_index, current):
        sub_start = step_index * step_rows
        key_part = lax.dynamic_slice_in_dim(key_piece, sub_start, step_rows, 0)
        value_part = lax.dynamic_slice_in_dim(value_piece, sub_start, step_rows, 0)
        return block_update(
            current, queries, query_pos, key_part, value_part, sub_start, score_scale
        )

    return lax.fori_loop(0, count_rows // step_rows, one_step, carried)


def finish(carried):
    run_max, run_sum, run_acc = carried
    normed = run_acc / run_sum[:, :, None]
    heads_here, rows_here, depth = normed.shape
    return (
        jnp.transpose(normed, (1, 0, 2)).reshape(rows_here, heads_here * depth).astype(jnp.bfloat16)
    )


def local(
    gate_outer, gate_inner, value_in, pole_rates, pole_weights, skip_gain, query_rows, key_rows
):
    tok_rows, width = gate_outer.shape
    poles_here = pole_rates.shape[0]
    seq_index = lax.axis_index("seq")
    chan_count = lax.axis_size("chan")
    gated = gate_inner.astype(jnp.float32) * value_in.astype(jnp.float32)
    offsets = jnp.arange(tok_rows, dtype=jnp.float32)
    growth = jnp.exp(offsets[:, None, None] * pole_rates[None, :, :])
    weighted = growth * gated[:, None, :]
    lower = (jnp.arange(tok_rows)[:, None] >= jnp.arange(tok_rows)[None, :]).astype(jnp.float32)
    running = jnp.dot(
        lower, weighted.reshape(tok_rows, poles_here * width), precision=lax.Precision.HIGHEST
    )
    running = running.reshape(tok_rows, poles_here, width)
    block_span = jnp.float32(tok_rows)
    summary = running[-1] * jnp.exp(-(block_span - 1.0) * pole_rates)

    def chain_states(earlier, later):
        fade = jnp.exp(-block_span * later[1] * pole_rates)
        return (later[0] + fade * earlier[0], earlier[1] + later[1])

    identity = (jnp.zeros_like(summary), jnp.zeros((1, 1), jnp.float32))
    carry_in, block_count = prefix(
        (summary, jnp.ones((1, 1), jnp.float32)), "seq", chain_states, identity
    )
    decayed = jnp.exp(-offsets[:, None, None] * pole_rates[None, :, :])
    modal = decayed * (running + (jnp.exp(-pole_rates) * carry_in)[None, :, :])
    filtered = jnp.sum(modal * (pole_weights * jnp.sqrt(pole_rates))[None, :, :], axis=1)
    conv_out = gate_outer.astype(jnp.float32) * (filtered + skip_gain[None, :] * gated)
    local_squares = jnp.sum(conv_out * conv_out, axis=1)
    total_squares = lax.psum(local_squares, "chan")
    mean_square = total_squares / (width * chan_count)
    values = (conv_out * lax.rsqrt(mean_square[:, None] + 1e-06)).astype(jnp.bfloat16)
    score_scale = HD ** (-0.5)
    heads_here = width // HD
    my_start = seq_index * tok_rows
    all_pos = my_start + jnp.arange(tok_rows, dtype=jnp.int32)
    final_state = fold_keys(
        (
            jnp.full((heads_here, tok_rows), -1e30, jnp.float32),
            jnp.zeros((heads_here, tok_rows), jnp.float32),
            jnp.zeros((heads_here, tok_rows, HD), jnp.float32),
        ),
        query_rows,
        all_pos,
        (
            lax.all_gather(key_rows, "seq", axis=0, tiled=True),
            lax.all_gather(values, "seq", axis=0, tiled=True),
        ),
        score_scale,
    )
    mixed = finish(final_state)
    return mixed


def solution(mesh):
    in_specs = (
        P("seq", "chan"),
        P("seq", "chan"),
        P("seq", "chan"),
        P(None, "chan"),
        P(None, "chan"),
        P("chan"),
        P("seq", "chan"),
        P("seq", "chan"),
    )
    out_specs = P("seq", "chan")
    return jax.shard_map(local, mesh=mesh, in_specs=in_specs, out_specs=out_specs, check_vma=False)
```

profile of v0, /device:TPU:1, one launch (start us, length us, event | category | flops | bytes accessed | tf_op | source)
XLA Modules:
  0.0 426.7 jit_solution(17308309685470993890)
XLA Ops:
  6.5 0.7 copy.35
  7.3 1.0 convert_multiply_fusion
  8.5 1.6 copy.36
  10.2 1.6 fusion.21
  12.5 0.8 copy.26
  13.4 3.0 copy.37
  16.4 1.3 dynamic-slice
  17.7 0.7 dynamic-update-slice
  18.5 130.3 %all-reduce = f32[64]{0:T(128)S(1)} all-reduce(f32[64]{0:T(128)S(1)} %dynamic-update-slice), channel_id=1, replica_groups=mesh['seq'=64,'chan'=8] {'seq'}, use_global_device_ids=true, to_apply=%add | all-reduce | flops 64 | bytes 512
  148.8 2.0 while.30
  149.5 1.4 bitcast_add_fusion.3
  150.9 2.6 fusion.20
  153.7 16.0 %psum.7 = f32[128]{0:T(128)S(1)} all-reduce(f32[128]{0:T(128)S(1)} %multiply_reduce_fusion), channel_id=1, replica_groups=mesh['seq'=64,'chan'=8] {'chan'}, use_global_device_ids=true, to_apply=%region_4.5 | all-reduce | flops 128 | bytes 1024 | tf_op jit(solution)/shard_map/psum | solution.py:104
  169.7 0.7 multiply_convert_fusion
  170.5 21.5 %all-gather.5.cloned.1.call-done = bf16[8192,512]{0,1:T(8,128)(2,1)} async-done(((bf16[128,512]{0,1:T(8,128)(2,1)}), bf16[8192,512]{0,1:T(8,128)(2,1)}) %all-gather.5.cloned.1.call-update) | async-done | bytes 8388624 | tf_op jit(solution)/shard_map/all_gather | solution.py:120
  192.0 183.1 %all-gather.7.cloned.1.call-done = bf16[8192,512]{1,0:T(8,128)(2,1)} async-done(((bf16[128,512]{1,0:T(8,128)(2,1)}), bf16[8192,512]{1,0:T(8,128)(2,1)}) %all-gather.7.cloned.1.call-update) | async-done | bytes 8388624 | tf_op jit(solution)/shard_map/all_gather | solution.py:121
  375.1 44.3 %while.31 = (s32[]{:T(128)}, f32[4,128]{1,0:T(4,128)S(1)}, f32[4,128]{1,0:T(4,128)S(1)}, f32[4,128,128]{2,1,0:T(8,128)S(1)}, bf16[8192,512]{0,1:T(8,128)(2,1)}, ...) while((s32[]{:T(128)}, f32[4,128]{1,0:T(4,128)S(1)}, ...), condition=%wide.region_8.9_spmd.clone, body=%wide.region_5.8_spmd.clone.sunk | while | flops 275582592 | bytes 15901895 | solution.py:60
  375.3 1.3 constant_dynamic-slice_fusion.6
  377.2 1.3 constant_dynamic-slice_fusion.5
  378.5 0.6 fusion.46
  379.7 0.9 convolution_add_fusion.2
  380.9 1.3 constant_dynamic-slice_fusion.6
  382.7 1.3 constant_dynamic-slice_fusion.5
  384.0 0.6 fusion.46
  385.2 0.9 convolution_add_fusion.2
  386.4 1.3 constant_dynamic-slice_fusion.6
  388.2 1.3 constant_dynamic-slice_fusion.5
  389.5 0.6 fusion.46
  390.7 0.9 convolution_add_fusion.2
  391.9 1.3 constant_dynamic-slice_fusion.6
  393.8 1.3 constant_dynamic-slice_fusion.5
  395.1 0.6 fusion.46
  396.3 0.9 convolution_add_fusion.2
  397.5 1.3 constant_dynamic-slice_fusion.6
  399.3 1.3 constant_dynamic-slice_fusion.5
  400.6 0.6 fusion.46
  401.8 0.9 convolution_add_fusion.2
  403.0 1.3 constant_dynamic-slice_fusion.6
  404.9 1.3 constant_dynamic-slice_fusion.5
  407.4 0.9 convolution_add_fusion.2
  408.5 1.3 constant_dynamic-slice_fusion.6
  410.4 1.3 constant_dynamic-slice_fusion.5
  411.7 0.6 fusion.46
  412.9 0.9 convolution_add_fusion.2
  414.1 1.3 constant_dynamic-slice_fusion.6
  415.9 1.3 constant_dynamic-slice_fusion.5
  418.4 0.9 convolution_add_fusion.2
  419.4 0.8 copy_bitcast_fusion
  (103 shorter events, 13.7 us)
Async XLA Ops:
  6.5 142.3 %all-gather.9.cloned.1.call-start = ((), (), s32[]{:S(2)}) async-start(), calls=%async_computation.2 | async-start | bytes 1064960 | tf_op jit(solution)/shard_map/all_gather | solution.py:12
  10.2 1.7 copy-start.1
  10.2 2.3 copy-start.5
  12.5 179.6 %all-gather.5.cloned.1.call-start = ((), (), s32[]{:S(2)}) async-start(), calls=%async_computation | async-start | bytes 8519680 | tf_op jit(solution)/shard_map/all_gather | solution.py:120
  13.3 361.8 %all-gather.7.cloned.1.call-start = ((), (), s32[]{:S(2)}) async-start(), calls=%async_computation.1 | async-start | bytes 8519680 | tf_op jit(solution)/shard_map/all_gather | solution.py:121
  13.4 137.5 %copy-start.6 = (f32[8,512]{1,0:T(8,128)S(1)}, f32[8,512]{1,0:T(8,128)}, u32[]{:S(2)}) copy-start(f32[8,512]{1,0:T(8,128)} %param.16) | copy-start | bytes 49156
  16.4 137.1 %copy-start.2 = (bf16[128,512]{1,0:T(8,128)(2,1)S(1)}, bf16[128,512]{1,0:T(8,128)(2,1)}, u32[]{:S(2)}) copy-start(bf16[128,512]{1,0:T(8,128)(2,1)} %param.14) | copy-start | bytes 393220
  16.4 137.1 %copy-start.3 = (bf16[128,512]{1,0:T(8,128)(2,1)S(1)}, bf16[128,512]{1,0:T(8,128)(2,1)}, u32[]{:S(2)}) copy-start(bf16[128,512]{1,0:T(8,128)(2,1)} %param.13) | copy-start | bytes 393220
  16.4 137.1 %copy-start.4 = (bf16[128,512]{1,0:T(8,128)(2,1)S(1)}, bf16[128,512]{1,0:T(8,128)(2,1)}, u32[]{:S(2)}) copy-start(bf16[128,512]{1,0:T(8,128)(2,1)} %param.12) | copy-start | bytes 393220
  16.4 137.1 %copy-start.7 = (f32[512]{0:T(512)S(1)}, f32[512]{0:T(512)}, u32[]{:S(2)}) copy-start(f32[512]{0:T(512)} %param.17) | copy-start | bytes 6148
  150.9 224.2 %copy-start = (bf16[128,512]{1,0:T(8,128)(2,1)S(1)}, bf16[128,512]{1,0:T(8,128)(2,1)}, u32[]{:S(2)}) copy-start(bf16[128,512]{1,0:T(8,128)(2,1)} %param.18) | copy-start | bytes 393220
Sparse Core Ops, SparseCore 0:
  12.6 87.8 all-gather.8
  103.6 88.3 all-gather.4
  195.4 179.6 all-gather.6
where the time goes:
time: 433 us; the launch traced here: 427 us
  waiting for transfers between devices  205 us (47%)
  blocking collectives  146 us (34%)
  local copies, waits for them, and re-layouts  33.7 us (8%)
  other arithmetic  14.1 us (3%)
  matrix products  13.9 us (3%)
  between operations  13.3 us (3%)
    all_gather x1, waiting for transfers between devices, local(): lax.all_gather(values, 'seq', axis=0, tiled=True)  183 us
    unnamed x1, blocking collectives  130 us
    all_gather x1, waiting for transfers between devices, local(): lax.all_gather(key_rows, 'seq', axis=0, tiled=True)  21.5 us
    psum x1, blocking collectives, local(): total_squares = lax.psum(local_squares, 'chan')  16 us
    dynamic_slice x16, local copies, waits for them, and re-layouts, one_step(): value_part = lax.dynamic_slice_in_dim(value_piece, sub_start, step_rows, 0)  14.7 us
    dynamic_slice x8, local copies, waits for them, and re-layouts, one_step(): key_part = lax.dynamic_slice_in_dim(key_piece, sub_start, step_rows, 0)  10.4 us
  transfers between devices with their start and end apart: 3, of which 2 were waited for; matrix products, arithmetic and copies ran while one was open for 3% of the time, Pallas kernels for 0%

commit v1 on v0

--- a/solution.py
+++ b/solution.py
@@ -101,7 +101,11 @@
     filtered = jnp.sum(modal * (pole_weights * jnp.sqrt(pole_rates))[None, :, :], axis=1)
     conv_out = gate_outer.astype(jnp.float32) * (filtered + skip_gain[None, :] * gated)
     local_squares = jnp.sum(conv_out * conv_out, axis=1)
-    total_squares = lax.psum(local_squares, "chan")
+    total_squares = local_squares
+    for hop in (1, 2, 4):
+        total_squares = total_squares + lax.ppermute(
+            total_squares, "chan", [(dev, dev ^ hop) for dev in range(8)]
+        )
     mean_square = total_squares / (width * chan_count)
     values = (conv_out * lax.rsqrt(mean_square[:, None] + 1e-06)).astype(jnp.bfloat16)
     score_scale = HD ** (-0.5)

time: 433 us -> 440 us (1.016)
  blocking collectives: 146 us -> 130 us
  waiting for transfers between devices: 205 us -> 218 us
  starting transfers between devices: 0.09 us -> 9.82 us
    psum x1 -> x0, blocking collectives: 16 us -> none  [local(): total_squares = lax.psum(local_squares, 'chan')]
    ppermute x0 -> x3, starting transfers between devices: none -> 9.74 us  [local(): lax.ppermute(total_squares, 'chan', [(dev, dev ^ hop) for dev in range(8)])]
    ppermute x0 -> x3, waiting for transfers between devices: none -> 8.75 us  [local(): lax.ppermute(total_squares, 'chan', [(dev, dev ^ hop) for dev in range(8)])]
    all_gather x1, waiting for transfers between devices: 183 us -> 189 us  [local(): lax.all_gather(values, 'seq', axis=0, tiled=True)]
  transfers between devices with their start and end apart: 3 -> 6, of which waited for: 2 -> 5; matrix products, arithmetic and copies ran while one was open for 3% -> 3% of each run, Pallas kernels for 0% -> 0%
where the time goes in v1:
time: 440 us; the launch traced here: 433 us
  waiting for transfers between devices  218 us (50%)
  blocking collectives  130 us (30%)
  local copies, waits for them, and re-layouts  33.6 us (8%)
  other arithmetic  14.1 us (3%)
  matrix products  13.9 us (3%)
  between operations  13.4 us (3%)
  starting transfers between devices  9.82 us (2%)
    all_gather x1, waiting for transfers between devices, local(): lax.all_gather(values, 'seq', axis=0, tiled=True)  189 us
    unnamed x1, blocking collectives  130 us
    all_gather x1, waiting for transfers between devices, local(): lax.all_gather(key_rows, 'seq', axis=0, tiled=True)  19.3 us
    dynamic_slice x16, local copies, waits for them, and re-layouts, one_step(): value_part = lax.dynamic_slice_in_dim(value_piece, sub_start, step_rows, 0)  14.7 us
    dynamic_slice x8, local copies, waits for them, and re-layouts, one_step(): key_part = lax.dynamic_slice_in_dim(key_piece, sub_start, step_rows, 0)  10.4 us
    ppermute x3, starting transfers between devices, local(): lax.ppermute(total_squares, 'chan', [(dev, dev ^ hop) for dev in range(8)])  9.74 us
  transfers between devices with their start and end apart: 6, of which 5 were waited for; matrix products, arithmetic and copies ran while one was open for 3% of the time, Pallas kernels for 0%

profile of v1, /device:TPU:1, one launch (start us, length us, event | category | flops | bytes accessed | tf_op | source)
XLA Modules:
  0.0 433.3 jit_solution(5424454973071448094)
XLA Ops:
  6.5 0.7 copy.35
  7.3 1.0 convert_multiply_fusion
  8.5 1.6 copy.36
  10.2 1.6 fusion.21
  12.5 0.8 copy.26
  13.4 3.0 copy.37
  16.4 1.3 dynamic-slice
  17.7 0.7 dynamic-update-slice
  18.4 130.2 %all-reduce = f32[64]{0:T(128)S(1)} all-reduce(f32[64]{0:T(128)S(1)} %dynamic-update-slice), channel_id=1, replica_groups=mesh['seq'=64,'chan'=8] {'seq'}, use_global_device_ids=true, to_apply=%add | all-reduce | flops 64 | bytes 512
  148.7 2.0 while.30
  148.7 0.6 fusion.41
  149.3 1.4 bitcast_add_fusion.3
  150.7 2.6 fusion.20
  153.5 1.9 collective-permute-start
  155.5 2.8 collective-permute-done
  158.3 1.9 collective-permute-start.1
  160.2 3.7 collective-permute-done.1
  163.9 5.9 %collective-permute-start.2 = (f32[128]{0:T(128)S(1)}, f32[128]{0:T(128)S(1)}, u32[]{:S(2)}, u32[]{:S(2)}) collective-permute-start(f32[128]{0:T(128)S(1)} %add.109), channel_id=1, source_target_pairs={{0,4},{1,5},{2,6},{3,7},{4,0},{5,1},{6,2},{7,3},{8,12},{9,13},{10,... | collective-permute-start | bytes 1544 | tf_op jit(solution)/shard_map/ppermute | solution.py:106
  169.8 2.3 collective-permute-done.2
  172.1 0.8 multiply_convert_fusion
  172.9 19.3 %all-gather.5.cloned.1.call-done = bf16[8192,512]{0,1:T(8,128)(2,1)} async-done(((bf16[128,512]{0,1:T(8,128)(2,1)}), bf16[8192,512]{0,1:T(8,128)(2,1)}) %all-gather.5.cloned.1.call-update) | async-done | bytes 8388624 | tf_op jit(solution)/shard_map/all_gather | solution.py:124
  192.2 189.5 %all-gather.7.cloned.1.call-done = bf16[8192,512]{1,0:T(8,128)(2,1)} async-done(((bf16[128,512]{1,0:T(8,128)(2,1)}), bf16[8192,512]{1,0:T(8,128)(2,1)}) %all-gather.7.cloned.1.call-update) | async-done | bytes 8388624 | tf_op jit(solution)/shard_map/all_gather | solution.py:125
  381.7 44.3 %while.31 = (s32[]{:T(128)}, f32[4,128]{1,0:T(4,128)S(1)}, f32[4,128]{1,0:T(4,128)S(1)}, f32[4,128,128]{2,1,0:T(8,128)S(1)}, bf16[8192,512]{0,1:T(8,128)(2,1)}, ...) while((s32[]{:T(128)}, f32[4,128]{1,0:T(4,128)S(1)}, ...), condition=%wide.region_7.8_spmd.clone, body=%wide.region_4.7_spmd.clone.sunk | while | flops 275582592 | bytes 15901895 | solution.py:60
  381.9 1.3 constant_dynamic-slice_fusion.6
  383.8 1.3 constant_dynamic-slice_fusion.5
  386.3 0.9 convolution_add_fusion.2
  387.5 1.3 constant_dynamic-slice_fusion.6
  389.3 1.3 constant_dynamic-slice_fusion.5
  391.8 0.9 convolution_add_fusion.2
  393.0 1.3 constant_dynamic-slice_fusion.6
  394.9 1.3 constant_dynamic-slice_fusion.5
  397.4 0.9 convolution_add_fusion.2
  398.6 1.3 constant_dynamic-slice_fusion.6
  400.4 1.3 constant_dynamic-slice_fusion.5
  402.9 0.9 convolution_add_fusion.2
  404.1 1.3 constant_dynamic-slice_fusion.6
  405.9 1.3 constant_dynamic-slice_fusion.5
  408.4 0.9 convolution_add_fusion.2
  409.6 1.3 constant_dynamic-slice_fusion.6
  411.5 1.3 constant_dynamic-slice_fusion.5
  414.0 0.9 convolution_add_fusion.2
  415.2 1.3 constant_dynamic-slice_fusion.6
  417.0 1.3 constant_dynamic-slice_fusion.5
  419.5 0.9 convolution_add_fusion.2
  420.7 1.3 constant_dynamic-slice_fusion.6
  422.6 1.3 constant_dynamic-slice_fusion.5
  425.1 0.9 convolution_add_fusion.2
  426.0 0.8 copy_bitcast_fusion
  (110 shorter events, 16.9 us)
Async XLA Ops:
  6.5 142.1 %all-gather.9.cloned.1.call-start = ((), (), s32[]{:S(2)}) async-start(), calls=%async_computation.2 | async-start | bytes 1064960 | tf_op jit(solution)/shard_map/all_gather | solution.py:12
  10.2 1.7 copy-start.1
  10.2 2.3 copy-start.5
  12.5 179.8 %all-gather.5.cloned.1.call-start = ((), (), s32[]{:S(2)}) async-start(), calls=%async_computation | async-start | bytes 8519680 | tf_op jit(solution)/shard_map/all_gather | solution.py:124
  13.3 368.4 %all-gather.7.cloned.1.call-start = ((), (), s32[]{:S(2)}) async-start(), calls=%async_computation.1 | async-start | bytes 8519680 | tf_op jit(solution)/shard_map/all_gather | solution.py:125
  13.4 137.3 %copy-start.6 = (f32[8,512]{1,0:T(8,128)S(1)}, f32[8,512]{1,0:T(8,128)}, u32[]{:S(2)}) copy-start(f32[8,512]{1,0:T(8,128)} %param.16) | copy-start | bytes 49156
  16.4 137.0 %copy-start.2 = (bf16[128,512]{1,0:T(8,128)(2,1)S(1)}, bf16[128,512]{1,0:T(8,128)(2,1)}, u32[]{:S(2)}) copy-start(bf16[128,512]{1,0:T(8,128)(2,1)} %param.14) | copy-start | bytes 393220
  16.4 137.0 %copy-start.3 = (bf16[128,512]{1,0:T(8,128)(2,1)S(1)}, bf16[128,512]{1,0:T(8,128)(2,1)}, u32[]{:S(2)}) copy-start(bf16[128,512]{1,0:T(8,128)(2,1)} %param.13) | copy-start | bytes 393220
  16.4 137.0 %copy-start.4 = (bf16[128,512]{1,0:T(8,128)(2,1)S(1)}, bf16[128,512]{1,0:T(8,128)(2,1)}, u32[]{:S(2)}) copy-start(bf16[128,512]{1,0:T(8,128)(2,1)} %param.12) | copy-start | bytes 393220
  16.4 137.0 %copy-start.7 = (f32[512]{0:T(512)S(1)}, f32[512]{0:T(512)}, u32[]{:S(2)}) copy-start(f32[512]{0:T(512)} %param.17) | copy-start | bytes 6148
  150.7 231.0 %copy-start = (bf16[128,512]{1,0:T(8,128)(2,1)S(1)}, bf16[128,512]{1,0:T(8,128)(2,1)}, u32[]{:S(2)}) copy-start(bf16[128,512]{1,0:T(8,128)(2,1)} %param.18) | copy-start | bytes 393220
  153.5 4.7 %collective-permute-start = (f32[128]{0:T(128)S(1)}, f32[128]{0:T(128)S(1)}, u32[]{:S(2)}, u32[]{:S(2)}) collective-permute-start(f32[128]{0:T(128)S(1)} %multiply_reduce_fusion), channel_id=1, source_target_pairs={{0,1},{1,0},{2,3},{3,2},{4,5},{5,4},{6,7},{7,6},{8,9},{9,8},{10,11... | collective-permute-start | bytes 1544 | tf_op jit(solution)/shard_map/ppermute | solution.py:106
  158.3 5.6 %collective-permute-start.1 = (f32[128]{0:T(128)S(1)}, f32[128]{0:T(128)S(1)}, u32[]{:S(2)}, u32[]{:S(2)}) collective-permute-start(f32[128]{0:T(128)S(1)} %add.108), channel_id=1, source_target_pairs={{0,2},{1,3},{2,0},{3,1},{4,6},{5,7},{6,4},{7,5},{8,10},{9,11},{10,... | collective-permute-start | bytes 1544 | tf_op jit(solution)/shard_map/ppermute | solution.py:106
  163.9 8.2 %collective-permute-start.2 = (f32[128]{0:T(128)S(1)}, f32[128]{0:T(128)S(1)}, u32[]{:S(2)}, u32[]{:S(2)}) collective-permute-start(f32[128]{0:T(128)S(1)} %add.109), channel_id=1, source_target_pairs={{0,4},{1,5},{2,6},{3,7},{4,0},{5,1},{6,2},{7,3},{8,12},{9,13},{10,... | collective-permute-start | bytes 1544 | tf_op jit(solution)/shard_map/ppermute | solution.py:106
Sparse Core Ops, SparseCore 0:
  12.6 87.8 all-gather.8
  103.6 88.5 all-gather.4
  195.6 186.0 all-gather.6
